TPU v7x, 32 devices: a whole 2x2x4 slice. The times are simulated.
32 devices in a mesh: epoch: 4 (over x, core), row: 8 (over z, y).
Axes of the slice: x: 2, y: 2, z: 4, core: 2. Of those that a mesh axis runs over, the one named last changes fastest.
Arguments:
- flux_image: float32 [16, 256, 1024], P('epoch', 'row'), may hold values from -8 to 8
- inv_var: float32 [16, 256, 1024], P('epoch', 'row'), may hold values from 0.5 to 4
- pixel_mask: int32 [16, 256, 1024], P('epoch', 'row'), may hold values 0 or 1
- psf_columns: float32 [16, 13], P('epoch'), may hold values from 0.02 to 0.3
- psf_rows: float32 [16, 13], P('epoch'), may hold values from 0.02 to 0.3
- epoch_times: int32 [16], P('epoch'), may hold values from 0 to 63, as said below
- trial_rates: int32 [4, 2], replicated, may hold values from -8 to 8, as said below
Outputs:
- psi_stack: float32 [4, 256, 1024], P('epoch', 'row')
- phi_stack: float32 [4, 256, 1024], P('epoch', 'row')
Inputs may be any that keep to these rules, and one draw needn't show every extreme that they name: `epoch_times`: some epoch has time index 0 and some has 63. `trial_rates`: some velocity has row rate 8 and some -8; some has column rate 8 and some -8.
All inputs are finite; a program needn't handle non-finite values. No bound on the sum of `pixel_mask` on one device may be relied on, other than what follows from the above.
Results may differ from a plain program's by a relative error of at most 0.00011.
Values sent between devices are 32-bit elements; how exact they have to be, the bound alone decides.
A program may use at most 64 MiB of HBM per device.

v0:
```python
import jax
import jax.numpy as jnp
from jax import lax
from jax.sharding import PartitionSpec as P

HALO = 8
PAD = 6
TSPAN = 64


def with_halo(array, sides, width):
    for axis, dim in sides:
        size, length = (lax.axis_size(axis), array.shape[dim])
        up = [(i, (i + 1) % size) for i in range(size - 1)]
        down = [(j, i) for i, j in up]
        last = lax.slice_in_dim(array, length - width, length, axis=dim)
        leading = lax.slice_in_dim(array, 0, width, axis=dim)
        before = lax.ppermute(last, axis, up)
        after = lax.ppermute(leading, axis, down)
        array = jnp.concatenate([before, array, after], axis=dim)
    return array


def conv_columns(fields_in, kernel):
    columns = fields_in.shape[3]
    padded = jnp.pad(fields_in, ((0, 0), (0, 0), (0, 0), (PAD, PAD)))
    result = jnp.zeros(fields_in.shape, jnp.float32)
    for tap_index in range(2 * PAD + 1):
        result = (
            result
            + kernel[:, :, tap_index][:, :, None, None]
            * padded[:, :, :, tap_index : tap_index + columns]
        )
    return result


def conv_rows_valid(fields_in, kernel):
    out_rows = fields_in.shape[2] - 2 * PAD
    shape_out = (fields_in.shape[0], fields_in.shape[1], out_rows, fields_in.shape[3])
    result = jnp.zeros(shape_out, jnp.float32)
    for tap_index in range(2 * PAD + 1):
        result = (
            result
            + kernel[:, :, tap_index][:, :, None, None]
            * fields_in[:, :, tap_index : tap_index + out_rows, :]
        )
    return result


def inside_strip(field, row_first, rows_total, columns_total):
    row_place = row_first + jnp.arange(field.shape[2], dtype=jnp.int32)
    column_place = jnp.arange(field.shape[3], dtype=jnp.int32)
    row_good = (row_place >= 0) & (row_place < rows_total)
    column_good = (column_place >= 0) & (column_place < columns_total)
    keep = (row_good[:, None] & column_good[None, :]).astype(jnp.float32)
    return field * keep[None, None, :, :]


def shifted_sum(padded, row_starts, column_starts, out_rows):
    columns = padded.shape[3] - 2 * HALO

    def take_window(epoch_field, row_begin, column_begin):
        return lax.dynamic_slice(
            epoch_field, (jnp.int32(0), row_begin, column_begin), (2, out_rows, columns)
        )

    def one_velocity(starts):
        windows = jax.vmap(take_window)(padded, starts[0], starts[1])
        return jnp.sum(windows, axis=0)

    return lax.map(one_velocity, (jnp.transpose(row_starts), jnp.transpose(column_starts)))


def on_device(flux_image, inv_var, pixel_mask, psf_columns, psf_rows, epoch_times, trial_rates):
    weights = inv_var * pixel_mask.astype(jnp.float32)
    raw_fields = jnp.stack([flux_image * weights, weights], axis=1)
    own_rows = flux_image.shape[1]
    all_columns = flux_image.shape[2]
    rows_total = own_rows * lax.axis_size("row")
    row_block = lax.axis_index("row") * own_rows
    rim_width = HALO + PAD
    fields = conv_columns(raw_fields, jnp.stack([psf_columns, psf_columns * psf_columns], axis=1))
    row_kernel = jnp.stack([psf_rows, psf_rows * psf_rows], axis=1)
    row_shift = jnp.floor_divide(trial_rates[:, 0][None, :] * epoch_times[:, None], TSPAN)
    column_shift = jnp.floor_divide(trial_rates[:, 1][None, :] * epoch_times[:, None], TSPAN)
    row_starts = row_shift + HALO
    column_starts = column_shift + HALO
    widened = with_halo(fields, (("row", 2),), rim_width)
    convolved = conv_rows_valid(widened, row_kernel)
    convolved = inside_strip(convolved, row_block - HALO, rows_total, all_columns)
    padded = jnp.pad(convolved, ((0, 0), (0, 0), (0, 0), (HALO, HALO)))
    result = lax.psum_scatter(
        shifted_sum(padded, row_starts, column_starts, own_rows),
        "epoch",
        scatter_dimension=0,
        tiled=True,
    )
    return (result[:, 0], result[:, 1])


def solution(mesh):
    in_specs = (
        P("epoch", "row", None),
        P("epoch", "row", None),
        P("epoch", "row", None),
        P("epoch", None),
        P("epoch", None),
        P("epoch"),
        P(),
    )
    out_specs = (P("epoch", "row", None), P("epoch", "row", None))
    return jax.shard_map(
        on_device, mesh=mesh, in_specs=in_specs, out_specs=out_specs, check_vma=False
    )
```

profile of v0, /device:TPU:0, one launch (start us, length us, event | category | flops | bytes accessed | tf_op | source)
XLA Modules:
  0.0 130.9 jit_solution(13473098440953031683)
XLA Ops:
  12.9 3.6 %fusion.27 = f32[4,2,32,1024]{3,2,1,0:T(8,128)S(1)} fusion(f32[4,2,32,1024]{3,2,1,0:T(8,128)S(1)} %pad_maximum_fusion.1, f32[4,2]{1,0:T(4,128)S(1)} %bitcast.98, f32[4,2]{1,0:T(4,128)S(1)} %bitcast.97, f32[4,2]{1,0:T(4,128)S(1)} %bitcast.96, f32[4,2]{1,0:T(4,128)S(1)} %bitcast.95, f32[4,2]{1,0:T(4,128)S(1)} %bitcast.94, f32[4,2]{1,0:T(4,128)S(1)} %bitcast.93, ...), kind=kLoop, calls=%fused_computation.61 | loop fusion | flops 6553600 | bytes 2097568 | tf_op jit(solution)/shard_map/add | solution.py:30
  16.6 4.9 %collective-permute-start = (f32[4,2,14,1024]{3,2,1,0:T(8,128)S(1)}, f32[4,2,14,1024]{3,2,1,0:T(8,128)S(1)}, u32[]{:S(2)}, u32[]{:S(2)}) collective-permute-start(f32[4,2,14,1024]{3,2,1,0:T(8,128)S(1)} %get-tuple-element.69), channel_id=1, source_target_pairs={{0,1},{1,2},{2,3},{3,4},{4,5},{5,6},{6,7},{8,9},{9,10},{10,11},{11... | collective-permute-start | bytes 1376264 | tf_op jit(solution)/shard_map/ppermute | solution.py:18
  24.7 19.2 %collective-permute-done = f32[4,2,14,1024]{3,2,1,0:T(8,128)S(1)} collective-permute-done((f32[4,2,14,1024]{3,2,1,0:T(8,128)S(1)}, f32[4,2,14,1024]{3,2,1,0:T(8,128)S(1)}, u32[]{:S(2)}, u32[]{:S(2)}) %collective-permute-start) | collective-permute-done | bytes 458784 | tf_op jit(solution)/shard_map/ppermute | solution.py:18
  44.2 2.8 %fusion.3 = f32[4,2,48,1024]{3,2,1,0:T(8,128)S(1)} fusion(f32[4,2,60,1024]{3,2,1,0:T(8,128)S(1)} %pad_maximum_fusion, f32[48,1024]{1,0:T(8,128)S(1)} %and_convert_fusion, f32[4,2]{1,0:T(4,128)S(1)} %bitcast.85, f32[4,2]{1,0:T(4,128)S(1)} %bitcast.84, f32[4,2]{1,0:T(4,128)S(1)} %bitcast.83, f32[4,2]{1,0:T(4,128)S(1)} %bitcast.82, f32[4,2]{1,0:T(4,128)S(1)} %bitcast.80, ...), kind=kLoop, calls=%fused_computation.13 | loop fusion | flops 10223616 | bytes 22217120 | tf_op jit(solution)/shard_map/mul | solution.py:56
  47.5 47.8 %while.13 = (s32[]{:T(128)}, f32[4,2,32,1024]{3,2,1,0:T(8,128)}, s32[4,4]{1,0:T(4,128)S(1)}, s32[4,4]{1,0:T(4,128)S(1)}, f32[4,2,48,1040]{3,2,1,0:T(8,128)S(1)},...) while((s32[]{:T(128)}, f32[4,2,32,1024]{3,2,1,0:T(8,128)}, s32[4,4]{1,0:T(4,128)S(1)}, ...), condition=%wide.region_2.3_spmd, body=%wide.region_0.2_spmd.sunk | while | flops 196684 | bytes 2360450 | solution.py:71
  47.7 11.0 %while.14 = (s32[]{:T(128)}, f32[4,2,48,1040]{3,2,1,0:T(8,128)S(1)}, s32[4,4]{1,0:T(4,128)S(1)}, f32[4,2,32,1024]{3,2,1,0:T(8,128)S(1)}, s32[]{:T(128)}) while((s32[]{:T(128)}, f32[4,2,48,1040]{3,2,1,0:T(8,128)S(1)}, s32[4,4]{1,0:T(4,128)S(1)}, f32[4,2,32,1024]{3,2,1,0:T(8,128)S(1)}, s32[]{:T(128)}) %tuple.73), condition=%wide.while_cond, body=%wide.while_body.sunk | while | flops 2 | bytes 524425 | solution.py:63
  48.3 2.1 %dynamic-slice_dynamic-update-slice_fusion.2 = f32[4,2,32,1024]{3,2,1,0:T(8,128)S(1)} fusion(f32[4,2,32,1024]{3,2,1,0:T(8,128)S(1)} %get-tuple-element.190, s32[]{:T(128)} %get-tuple-element.187, f32[4,2,48,1040]{3,2,1,0:T(8,128)S(1)} %get-tuple-element.193, s32[]{:T(128)} %bitcast.66, s32[]{:T(128)} %bitcast.67, s32[]{:T(128)} %bitcast.68), kind=kLoop, calls=%fused_computation.clone.1 | loop fusion | bytes 524304 | tf_op jit(solution)/shard_map/while/body/eval_jaxpr/vmap()/gather
  51.1 2.1 %dynamic-slice_dynamic-update-slice_fusion.2 = f32[4,2,32,1024]{3,2,1,0:T(8,128)S(1)} fusion(f32[4,2,32,1024]{3,2,1,0:T(8,128)S(1)} %get-tuple-element.190, s32[]{:T(128)} %get-tuple-element.187, f32[4,2,48,1040]{3,2,1,0:T(8,128)S(1)} %get-tuple-element.193, s32[]{:T(128)} %bitcast.66, s32[]{:T(128)} %bitcast.67, s32[]{:T(128)} %bitcast.68), kind=kLoop, calls=%fused_computation.clone.1 | loop fusion | bytes 524304 | tf_op jit(solution)/shard_map/while/body/eval_jaxpr/vmap()/gather
  53.8 2.1 %dynamic-slice_dynamic-update-slice_fusion.2 = f32[4,2,32,1024]{3,2,1,0:T(8,128)S(1)} fusion(f32[4,2,32,1024]{3,2,1,0:T(8,128)S(1)} %get-tuple-element.190, s32[]{:T(128)} %get-tuple-element.187, f32[4,2,48,1040]{3,2,1,0:T(8,128)S(1)} %get-tuple-element.193, s32[]{:T(128)} %bitcast.66, s32[]{:T(128)} %bitcast.67, s32[]{:T(128)} %bitcast.68), kind=kLoop, calls=%fused_computation.clone.1 | loop fusion | bytes 524304 | tf_op jit(solution)/shard_map/while/body/eval_jaxpr/vmap()/gather
  56.6 2.1 %dynamic-slice_dynamic-update-slice_fusion.2 = f32[4,2,32,1024]{3,2,1,0:T(8,128)S(1)} fusion(f32[4,2,32,1024]{3,2,1,0:T(8,128)S(1)} %get-tuple-element.190, s32[]{:T(128)} %get-tuple-element.187, f32[4,2,48,1040]{3,2,1,0:T(8,128)S(1)} %get-tuple-element.193, s32[]{:T(128)} %bitcast.66, s32[]{:T(128)} %bitcast.67, s32[]{:T(128)} %bitcast.68), kind=kLoop, calls=%fused_computation.clone.1 | loop fusion | bytes 524304 | tf_op jit(solution)/shard_map/while/body/eval_jaxpr/vmap()/gather
  59.6 11.0 %while.14 = (s32[]{:T(128)}, f32[4,2,48,1040]{3,2,1,0:T(8,128)S(1)}, s32[4,4]{1,0:T(4,128)S(1)}, f32[4,2,32,1024]{3,2,1,0:T(8,128)S(1)}, s32[]{:T(128)}) while((s32[]{:T(128)}, f32[4,2,48,1040]{3,2,1,0:T(8,128)S(1)}, s32[4,4]{1,0:T(4,128)S(1)}, f32[4,2,32,1024]{3,2,1,0:T(8,128)S(1)}, s32[]{:T(128)}) %tuple.73), condition=%wide.while_cond, body=%wide.while_body.sunk | while | flops 2 | bytes 524425 | solution.py:63
  60.3 2.1 %dynamic-slice_dynamic-update-slice_fusion.2 = f32[4,2,32,1024]{3,2,1,0:T(8,128)S(1)} fusion(f32[4,2,32,1024]{3,2,1,0:T(8,128)S(1)} %get-tuple-element.190, s32[]{:T(128)} %get-tuple-element.187, f32[4,2,48,1040]{3,2,1,0:T(8,128)S(1)} %get-tuple-element.193, s32[]{:T(128)} %bitcast.66, s32[]{:T(128)} %bitcast.67, s32[]{:T(128)} %bitcast.68), kind=kLoop, calls=%fused_computation.clone.1 | loop fusion | bytes 524304 | tf_op jit(solution)/shard_map/while/body/eval_jaxpr/vmap()/gather
  63.0 2.1 %dynamic-slice_dynamic-update-slice_fusion.2 = f32[4,2,32,1024]{3,2,1,0:T(8,128)S(1)} fusion(f32[4,2,32,1024]{3,2,1,0:T(8,128)S(1)} %get-tuple-element.190, s32[]{:T(128)} %get-tuple-element.187, f32[4,2,48,1040]{3,2,1,0:T(8,128)S(1)} %get-tuple-element.193, s32[]{:T(128)} %bitcast.66, s32[]{:T(128)} %bitcast.67, s32[]{:T(128)} %bitcast.68), kind=kLoop, calls=%fused_computation.clone.1 | loop fusion | bytes 524304 | tf_op jit(solution)/shard_map/while/body/eval_jaxpr/vmap()/gather
  65.8 2.1 %dynamic-slice_dynamic-update-slice_fusion.2 = f32[4,2,32,1024]{3,2,1,0:T(8,128)S(1)} fusion(f32[4,2,32,1024]{3,2,1,0:T(8,128)S(1)} %get-tuple-element.190, s32[]{:T(128)} %get-tuple-element.187, f32[4,2,48,1040]{3,2,1,0:T(8,128)S(1)} %get-tuple-element.193, s32[]{:T(128)} %bitcast.66, s32[]{:T(128)} %bitcast.67, s32[]{:T(128)} %bitcast.68), kind=kLoop, calls=%fused_computation.clone.1 | loop fusion | bytes 524304 | tf_op jit(solution)/shard_map/while/body/eval_jaxpr/vmap()/gather
  68.5 2.1 %dynamic-slice_dynamic-update-slice_fusion.2 = f32[4,2,32,1024]{3,2,1,0:T(8,128)S(1)} fusion(f32[4,2,32,1024]{3,2,1,0:T(8,128)S(1)} %get-tuple-element.190, s32[]{:T(128)} %get-tuple-element.187, f32[4,2,48,1040]{3,2,1,0:T(8,128)S(1)} %get-tuple-element.193, s32[]{:T(128)} %bitcast.66, s32[]{:T(128)} %bitcast.67, s32[]{:T(128)} %bitcast.68), kind=kLoop, calls=%fused_computation.clone.1 | loop fusion | bytes 524304 | tf_op jit(solution)/shard_map/while/body/eval_jaxpr/vmap()/gather
  71.5 11.0 %while.14 = (s32[]{:T(128)}, f32[4,2,48,1040]{3,2,1,0:T(8,128)S(1)}, s32[4,4]{1,0:T(4,128)S(1)}, f32[4,2,32,1024]{3,2,1,0:T(8,128)S(1)}, s32[]{:T(128)}) while((s32[]{:T(128)}, f32[4,2,48,1040]{3,2,1,0:T(8,128)S(1)}, s32[4,4]{1,0:T(4,128)S(1)}, f32[4,2,32,1024]{3,2,1,0:T(8,128)S(1)}, s32[]{:T(128)}) %tuple.73), condition=%wide.while_cond, body=%wide.while_body.sunk | while | flops 2 | bytes 524425 | solution.py:63
  74.9 2.1 %dynamic-slice_dynamic-update-slice_fusion.2 = f32[4,2,32,1024]{3,2,1,0:T(8,128)S(1)} fusion(f32[4,2,32,1024]{3,2,1,0:T(8,128)S(1)} %get-tuple-element.190, s32[]{:T(128)} %get-tuple-element.187, f32[4,2,48,1040]{3,2,1,0:T(8,128)S(1)} %get-tuple-element.193, s32[]{:T(128)} %bitcast.66, s32[]{:T(128)} %bitcast.67, s32[]{:T(128)} %bitcast.68), kind=kLoop, calls=%fused_computation.clone.1 | loop fusion | bytes 524304 | tf_op jit(solution)/shard_map/while/body/eval_jaxpr/vmap()/gather
  77.7 2.1 %dynamic-slice_dynamic-update-slice_fusion.2 = f32[4,2,32,1024]{3,2,1,0:T(8,128)S(1)} fusion(f32[4,2,32,1024]{3,2,1,0:T(8,128)S(1)} %get-tuple-element.190, s32[]{:T(128)} %get-tuple-element.187, f32[4,2,48,1040]{3,2,1,0:T(8,128)S(1)} %get-tuple-element.193, s32[]{:T(128)} %bitcast.66, s32[]{:T(128)} %bitcast.67, s32[]{:T(128)} %bitcast.68), kind=kLoop, calls=%fused_computation.clone.1 | loop fusion | bytes 524304 | tf_op jit(solution)/shard_map/while/body/eval_jaxpr/vmap()/gather
  80.4 2.1 %dynamic-slice_dynamic-update-slice_fusion.2 = f32[4,2,32,1024]{3,2,1,0:T(8,128)S(1)} fusion(f32[4,2,32,1024]{3,2,1,0:T(8,128)S(1)} %get-tuple-element.190, s32[]{:T(128)} %get-tuple-element.187, f32[4,2,48,1040]{3,2,1,0:T(8,128)S(1)} %get-tuple-element.193, s32[]{:T(128)} %bitcast.66, s32[]{:T(128)} %bitcast.67, s32[]{:T(128)} %bitcast.68), kind=kLoop, calls=%fused_computation.clone.1 | loop fusion | bytes 524304 | tf_op jit(solution)/shard_map/while/body/eval_jaxpr/vmap()/gather
  83.5 11.0 %while.14 = (s32[]{:T(128)}, f32[4,2,48,1040]{3,2,1,0:T(8,128)S(1)}, s32[4,4]{1,0:T(4,128)S(1)}, f32[4,2,32,1024]{3,2,1,0:T(8,128)S(1)}, s32[]{:T(128)}) while((s32[]{:T(128)}, f32[4,2,48,1040]{3,2,1,0:T(8,128)S(1)}, s32[4,4]{1,0:T(4,128)S(1)}, f32[4,2,32,1024]{3,2,1,0:T(8,128)S(1)}, s32[]{:T(128)}) %tuple.73), condition=%wide.while_cond, body=%wide.while_body.sunk | while | flops 2 | bytes 524425 | solution.py:63
  84.1 2.1 %dynamic-slice_dynamic-update-slice_fusion.2 = f32[4,2,32,1024]{3,2,1,0:T(8,128)S(1)} fusion(f32[4,2,32,1024]{3,2,1,0:T(8,128)S(1)} %get-tuple-element.190, s32[]{:T(128)} %get-tuple-element.187, f32[4,2,48,1040]{3,2,1,0:T(8,128)S(1)} %get-tuple-element.193, s32[]{:T(128)} %bitcast.66, s32[]{:T(128)} %bitcast.67, s32[]{:T(128)} %bitcast.68), kind=kLoop, calls=%fused_computation.clone.1 | loop fusion | bytes 524304 | tf_op jit(solution)/shard_map/while/body/eval_jaxpr/vmap()/gather
  89.6 2.1 %dynamic-slice_dynamic-update-slice_fusion.2 = f32[4,2,32,1024]{3,2,1,0:T(8,128)S(1)} fusion(f32[4,2,32,1024]{3,2,1,0:T(8,128)S(1)} %get-tuple-element.190, s32[]{:T(128)} %get-tuple-element.187, f32[4,2,48,1040]{3,2,1,0:T(8,128)S(1)} %get-tuple-element.193, s32[]{:T(128)} %bitcast.66, s32[]{:T(128)} %bitcast.67, s32[]{:T(128)} %bitcast.68), kind=kLoop, calls=%fused_computation.clone.1 | loop fusion | bytes 524304 | tf_op jit(solution)/shard_map/while/body/eval_jaxpr/vmap()/gather
  92.4 2.1 %dynamic-slice_dynamic-update-slice_fusion.2 = f32[4,2,32,1024]{3,2,1,0:T(8,128)S(1)} fusion(f32[4,2,32,1024]{3,2,1,0:T(8,128)S(1)} %get-tuple-element.190, s32[]{:T(128)} %get-tuple-element.187, f32[4,2,48,1040]{3,2,1,0:T(8,128)S(1)} %get-tuple-element.193, s32[]{:T(128)} %bitcast.66, s32[]{:T(128)} %bitcast.67, s32[]{:T(128)} %bitcast.68), kind=kLoop, calls=%fused_computation.clone.1 | loop fusion | bytes 524304 | tf_op jit(solution)/shard_map/while/body/eval_jaxpr/vmap()/gather
  95.3 27.1 %reduce-scatter.2.cloned.1.call-done = f32[1,2,32,1024]{3,2,1,0:T(8,128)} async-done(((f32[4,2,32,1024]{3,2,1,0:T(8,128)}), f32[1,2,32,1024]{3,2,1,0:T(8,128)}) %reduce-scatter.2.cloned.1.call-update) | async-done | bytes 262160 | tf_op jit(solution)/shard_map/reduce_scatter | solution.py:92
  (120 shorter events, 29.8 us)
Async XLA Ops:
  7.2 115.2 %reduce-scatter.2.cloned.1.call-start = ((), (), s32[]{:S(2)}) async-start(), calls=%async_computation.1 | async-start | bytes 1310720 | tf_op jit(solution)/shard_map/reduce_scatter | solution.py:92
  16.5 6.4 %copy-start = (f32[4,13]{1,0:T(4,128)S(1)}, f32[4,13]{1,0:T(4,128)}, u32[]{:S(2)}) copy-start(f32[4,13]{1,0:T(4,128)} %param.13) | copy-start | bytes 628
  16.5 6.6 %copy-start.1 = (s32[4,2]{0,1:T(2,128)S(1)}, s32[4,2]{0,1:T(2,128)}, u32[]{:S(2)}) copy-start(s32[4,2]{0,1:T(2,128)} %param.15) | copy-start | bytes 100
  16.5 8.0 %copy-start.2 = (s32[4]{0:T(128)S(1)}, s32[4]{0:T(128)}, u32[]{:S(2)}) copy-start(s32[4]{0:T(128)} %param.14) | copy-start | bytes 52
  16.6 27.3 %collective-permute-start = (f32[4,2,14,1024]{3,2,1,0:T(8,128)S(1)}, f32[4,2,14,1024]{3,2,1,0:T(8,128)S(1)}, u32[]{:S(2)}, u32[]{:S(2)}) collective-permute-start(f32[4,2,14,1024]{3,2,1,0:T(8,128)S(1)} %get-tuple-element.69), channel_id=1, source_target_pairs={{0,1},{1,2},{2,3},{3,4},{4,5},{5,6},{6,7},{8,9},{9,10},{10,11},{11... | collective-permute-start | bytes 1376264 | tf_op jit(solution)/shard_map/ppermute | solution.py:18
  21.6 22.4 %collective-permute-start.1 = (f32[4,2,14,1024]{3,2,1,0:T(8,128)S(1)}, f32[4,2,14,1024]{3,2,1,0:T(8,128)S(1)}, u32[]{:S(2)}, u32[]{:S(2)}) collective-permute-start(f32[4,2,14,1024]{3,2,1,0:T(8,128)S(1)} %get-tuple-element.70), channel_id=1, source_target_pairs={{1,0},{2,1},{3,2},{4,3},{5,4},{6,5},{7,6},{9,8},{10,9},{11,10},{12... | collective-permute-start | bytes 1376264 | tf_op jit(solution)/shard_map/ppermute | solution.py:19
Sparse Core Ops, SparseCore 0:
  95.4 26.9 reduce-scatter.1
where the time goes:
time: 132 us; the launch traced here: 131 us
  local copies, waits for them, and re-layouts  52 us (39%)
  waiting for transfers between devices  46.3 us (35%)
  between operations  14.2 us (11%)
  other arithmetic  11.6 us (9%)
  starting transfers between devices  6.26 us (5%)
    gather x48, local copies, waits for them, and re-layouts  43.5 us
    reduce_scatter x1, waiting for transfers between devices, on_device(): lax.psum_scatter(shifted_sum(padded, row_starts, column_starts, own_rows)...  27.1 us
    ppermute x1, waiting for transfers between devices, with_halo(): before = lax.ppermute(last, axis, up)  19.2 us
    ppermute x1, starting transfers between devices, with_halo(): before = lax.ppermute(last, axis, up)  4.93 us
    add x1, other arithmetic, conv_columns(): result + kernel[:, :, tap_index][:, :, None, None] * padded[:, :, :, tap_...  3.56 us
    dynamic_update_slice x4, local copies, waits for them, and re-layouts, shifted_sum(): lax.map(one_velocity, (jnp.transpose(row_starts), jnp.transpose(column_st...  2.93 us
    mul x1, other arithmetic, inside_strip(): return field * keep[None, None, :, :]  2.76 us
    another operation x3, other arithmetic, on_device(): jnp.stack([psf_columns, psf_columns * psf_columns], axis=1)  2.68 us
  transfers between devices with their start and end apart: 3, of which 2 were waited for; matrix products, arithmetic and copies ran while one was open for 1% of the time, Pallas kernels for 0%

commit v1 on v0

v1 whole, which is shorter than its diff:
```python
import functools

import jax
import jax.numpy as jnp
from jax import lax
from jax.experimental import pallas as pl
from jax.experimental.pallas import tpu as pltpu
from jax.sharding import PartitionSpec as P

HALO = 8
PAD = 6
TSPAN = 64
TAPS = 2 * PAD + 1
LANES = 128
NEAR = 8
OVER = 3 * NEAR
BAND = 2 * LANES
TALL = BAND + 2 * HALO
MESH = pl.DeviceIdType.MESH
F32 = jnp.float32
BF16 = jnp.bfloat16


def split(x):
    high = x.astype(BF16)
    return high, (x - high.astype(F32)).astype(BF16)


def iota(shape, axis):
    return lax.broadcasted_iota(jnp.int32, shape, axis)


def kernel(
    sizes,
    flux_hbm, inv_hbm, mask_hbm, psf_columns, psf_rows, times, rates,
    out_psi, out_phi,
    flux, inv, mask, toeplitz, padded, shifted,
    pair_out_over, pair_out_mid, pair_in_over, pair_in_mid,
    own_over, own_mid, far_in_over, far_in_mid,
    up_out, down_out, up_in, down_in,
    load_sem, pair_send, pair_recv, far_send, far_recv, row_send, row_recv,
):
    groups, row_devices = sizes
    epochs, rows, columns = flux.shape
    tiles = columns // LANES
    depth = epochs * rows
    me = lax.axis_index("epoch")
    core, group = lax.rem(me, 2), me // 2
    partner = me + 1 - 2 * core
    row = lax.axis_index("row")
    outs = (out_psi, out_phi)

    loads = []
    for e in range(epochs):
        for n, (src, dst) in enumerate(((inv_hbm, inv), (mask_hbm, mask), (flux_hbm, flux))):
            copy = pltpu.make_async_copy(src.at[e], dst.at[e], load_sem.at[e, n])
            copy.start()
            loads.append(copy)

    barrier = pltpu.get_barrier_semaphore()
    pl.semaphore_signal(barrier, inc=1, device_id={"epoch": partner}, device_id_type=MESH)
    for d in range(1, groups):
        there = 2 * lax.rem(group + d, groups) + core
        pl.semaphore_signal(barrier, inc=1, device_id={"epoch": there}, device_id_type=MESH)

    @pl.when(row > 0)
    def _():
        pl.semaphore_signal(barrier, inc=1, device_id={"row": row - 1}, device_id_type=MESH)

    @pl.when(row < row_devices - 1)
    def _():
        pl.semaphore_signal(barrier, inc=1, device_id={"row": row + 1}, device_id_type=MESH)

    offset = BAND // 4 - PAD + HALO
    lane = iota((NEAR, LANES), 1)
    place = iota((NEAR, LANES), 0) - lane
    wrapped = lax.rem(place - offset + 4 * LANES, LANES)
    for e in range(epochs):
        plain = jnp.zeros((NEAR, LANES), F32)
        for tap in range(TAPS):
            plain = jnp.where(wrapped == tap, psf_columns[e, tap], plain)
        for m in range(TALL // NEAR):
            turned = pltpu.roll(plain, (NEAR * m) % LANES, 1) if (NEAR * m) % LANES else plain
            where = place + (NEAR * m - offset)
            turned = jnp.where((where >= 0) & (where < TAPS), turned, 0.0)
            toeplitz[e, 0, m * NEAR : (m + 1) * NEAR, :] = turned
            toeplitz[e, 1, m * NEAR : (m + 1) * NEAR, :] = turned * turned

    half_lane = iota((rows, LANES), 1) < LANES // 2
    for e in range(epochs):
        for copy in loads[3 * e : 3 * e + 3]:
            copy.wait()
        weights = inv[e] * mask[e].astype(F32)
        for f, field in enumerate((flux[e] * weights, weights)):
            turned = pltpu.roll(field, LANES // 2, 1)
            first = turned[:, :LANES]
            for n, piece in enumerate(split(turned)):
                padded[e, f, n, :, LANES:columns] = piece[:, LANES:]
            for n, piece in enumerate(split(jnp.where(half_lane, 0.0, first))):
                padded[e, f, n, :, :LANES] = piece
            for n, piece in enumerate(split(jnp.where(half_lane, first, 0.0))):
                padded[e, f, n, :, columns:] = piece

    def shift(v, axis, e):
        return (rates[v, axis] * times[e]) >> (TSPAN.bit_length() - 1)

    def row_matrices(v):
        shape = (OVER + rows + NEAR, depth)
        o, k = iota(shape, 0), iota(shape, 1)
        far = jnp.where(rates[v, 0] >= 0, -2 * NEAR, rows + NEAR)
        r = jnp.where(o < NEAR, o - NEAR, rows + o - NEAR)
        r = jnp.where(o >= 2 * NEAR, o - 2 * NEAR + far, r)
        r = jnp.where(o >= OVER, o - OVER, r)
        epoch_of = k // rows
        step = jnp.zeros(shape, jnp.int32)
        for e in range(epochs):
            step = jnp.where(epoch_of == e, shift(v, 0, e), step)
        at = r + step
        good = (at + row * rows >= 0) & (at + row * rows < rows * row_devices) & (o < OVER + rows)
        tap_at = jnp.where(good, lax.rem(k, rows) - at + PAD, -1)
        one_row = epoch_of[:1]
        plain = jnp.zeros(shape, F32)
        for tap in range(TAPS):
            value = jnp.zeros((1, depth), F32)
            for e in range(epochs):
                value = jnp.where(one_row == e, psf_rows[e, tap], value)
            plain = jnp.where(tap_at == tap, value, plain)
        return split(plain), split(plain * plain)

    def columns_stage(pair, f):
        lanes = iota((rows, 2 * LANES), 1)
        for e in range(epochs):
            steps = [shift(v, 1, e) for v in pair]
            band = jnp.concatenate(
                [toeplitz[e, f, pl.ds(HALO - s, BAND), :] for s in steps], axis=1
            )
            band_high, band_low = split(band)
            high, low = (
                jnp.concatenate(
                    [padded[e, f, n, :, t * LANES : t * LANES + BAND] for t in range(tiles)], axis=0
                )
                for n in range(2)
            )
            result = jnp.dot(
                jnp.concatenate([high, low, high], axis=1),
                jnp.concatenate([band_high, band_high, band_low], axis=0),
                preferred_element_type=F32,
            )
            source = lax.rem(lanes, LANES) + jnp.where(lanes < LANES, steps[0], steps[1])
            for t in range(tiles):
                block = result[t * rows : (t + 1) * rows]
                if t == 0:
                    block = jnp.where(source >= 0, block, 0.0)
                if t == tiles - 1:
                    block = jnp.where(source + t * LANES < columns, block, 0.0)
                high_block, low_block = split(block)
                for h in range(2):
                    at = slice(t * LANES, (t + 1) * LANES)
                    part = slice(h * LANES, (h + 1) * LANES)
                    shifted[h, e * rows : (e + 1) * rows, at] = high_block[:, part]
                    shifted[h, depth + e * rows : depth + (e + 1) * rows, at] = low_block[:, part]

    def rows_stage(h, matrix):
        high, low = matrix
        return jnp.dot(
            jnp.concatenate([high, high], axis=1), shifted[h], preferred_element_type=F32
        ) + jnp.dot(low, shifted[h, :depth], preferred_element_type=F32)

    def pair_copy(d, f, part):
        src, dst = ((pair_out_over, pair_in_over), (pair_out_mid, pair_in_mid))[part]
        return pltpu.make_async_remote_copy(
            src_ref=src.at[d, f], dst_ref=dst.at[d, f],
            send_sem=pair_send.at[d, f, part], recv_sem=pair_recv.at[d, f, part],
            device_id={"epoch": partner}, device_id_type=MESH,
        )

    def far_copy(d, f, part):
        src, dst = ((own_over, far_in_over), (own_mid, far_in_mid))[part]
        return pltpu.make_async_remote_copy(
            src_ref=src.at[d, f], dst_ref=dst.at[d - 1, f],
            send_sem=far_send.at[d - 1, f, part], recv_sem=far_recv.at[d - 1, f, part],
            device_id={"epoch": 2 * lax.rem(group + d, groups) + core}, device_id_type=MESH,
        )

    def row_copy(f, way, other):
        src, dst = ((up_out, down_in), (down_out, up_in))[way]
        return pltpu.make_async_remote_copy(
            src_ref=src.at[f], dst_ref=dst.at[f],
            send_sem=row_send.at[f, way], recv_sem=row_recv.at[f, way],
            device_id={"row": other}, device_id_type=MESH,
        )

    def finish(d, f):
        for part, (own, arrived) in enumerate(((own_over, pair_in_over), (own_mid, pair_in_mid))):
            pair_copy(d, f, part).wait_recv()
            own[d, f] = own[d, f] + arrived[d, f]
            if d:
                far_copy(d, f, part).start()

    order = list(range(1, groups)) + [0]
    before = None
    for d in order:
        goal = 2 * lax.rem(group + d, groups)
        pair = (goal + 1 - core, goal + core)
        matrices = [row_matrices(v) for v in pair]
        for f in range(2):
            columns_stage(pair, f)
            if before is None:
                above = lax.div(row + row_devices - 1, row_devices)
                below = lax.div(2 * row_devices - 2 - row, row_devices)
                pl.semaphore_wait(barrier, groups + above + below)
            else:
                finish(*before)
            part = rows_stage(0, matrices[0][f])
            pair_out_over[d, f] = part[:OVER]
            pair_out_mid[d, f] = part[OVER : OVER + rows]
            pair_copy(d, f, 0).start()
            pair_copy(d, f, 1).start()
            part = rows_stage(1, matrices[1][f])
            own_over[d, f] = part[:OVER]
            own_mid[d, f] = part[OVER : OVER + rows]
            before = (d, f)
    finish(*before)

    upward = rates[me, 0] >= 0
    for f in range(2):
        total = own_over[0, f]
        for d in range(1, groups):
            far_copy(d, f, 0).wait_recv()
            total = total + far_in_over[d - 1, f]
        far = total[2 * NEAR :]
        up_out[f, :NEAR] = jnp.where(upward, far, 0.0)
        up_out[f, NEAR:] = total[:NEAR]
        down_out[f, :NEAR] = total[NEAR : 2 * NEAR]
        down_out[f, NEAR:] = jnp.where(upward, 0.0, far)

        @pl.when(row > 0)
        def _():
            row_copy(f, 0, row - 1).start()

        @pl.when(row < row_devices - 1)
        def _():
            row_copy(f, 1, row + 1).start()

        total = own_mid[0, f]
        for d in range(1, groups):
            far_copy(d, f, 1).wait_recv()
            total = total + far_in_mid[d - 1, f]
        outs[f][0] = total

    for f in range(2):
        @pl.when(row > 0)
        def _():
            row_copy(f, 1, row - 1).wait_recv()
            outs[f][0, : 2 * NEAR] = outs[f][0, : 2 * NEAR] + up_in[f]

        @pl.when(row < row_devices - 1)
        def _():
            row_copy(f, 0, row + 1).wait_recv()
            outs[f][0, rows - 2 * NEAR :] = outs[f][0, rows - 2 * NEAR :] + down_in[f]

    for f in range(2):
        for part in range(2):
            for d in range(groups):
                pair_copy(d, f, part).wait_send()
            for d in range(1, groups):
                far_copy(d, f, part).wait_send()

        @pl.when(row > 0)
        def _():
            row_copy(f, 0, row - 1).wait_send()

        @pl.when(row < row_devices - 1)
        def _():
            row_copy(f, 1, row + 1).wait_send()


def solution(mesh):
    epoch_devices, row_devices = mesh.shape["epoch"], mesh.shape["row"]
    groups = epoch_devices // 2

    def on_device(flux_image, inv_var, pixel_mask, psf_columns, psf_rows, epoch_times, trial_rates):
        epochs, rows, columns = flux_image.shape
        depth = epochs * rows
        assert epoch_devices % 2 == 0 and trial_rates.shape[0] == epoch_devices
        assert rows % (2 * NEAR) == 0 and columns % LANES == 0 and depth % LANES == 0
        far = max(groups - 1, 1)
        hbm = pl.BlockSpec(memory_space=pl.ANY)
        smem = pl.BlockSpec(memory_space=pltpu.SMEM)
        vmem = pl.BlockSpec(memory_space=pltpu.VMEM)
        image = (epochs, rows, columns)

        def pieces(count):
            return [
                pltpu.VMEM((count, 2, OVER, columns), F32),
                pltpu.VMEM((count, 2, rows, columns), F32),
            ]

        edge = pltpu.VMEM((2, 2 * NEAR, columns), F32)
        dma = pltpu.SemaphoreType.DMA
        return tuple(pl.pallas_call(
            functools.partial(kernel, (groups, row_devices)),
            out_shape=[jax.ShapeDtypeStruct((1, rows, columns), F32)] * 2,
            in_specs=[hbm] * 3 + [smem] * 4,
            out_specs=[vmem] * 2,
            scratch_shapes=[
                pltpu.VMEM(image, F32),
                pltpu.VMEM(image, F32),
                pltpu.VMEM(image, jnp.int32),
                pltpu.VMEM((epochs, 2, TALL, LANES), F32),
                pltpu.VMEM((epochs, 2, 2, rows, columns + LANES), BF16),
                pltpu.VMEM((2, 2 * depth, columns), BF16),
                *pieces(groups),
                *pieces(groups),
                *pieces(groups),
                *pieces(far),
                edge, edge, edge, edge,
                dma((epochs, 3)),
                dma((groups, 2, 2)),
                dma((groups, 2, 2)),
                dma((far, 2, 2)),
                dma((far, 2, 2)),
                dma((2, 2)),
                dma((2, 2)),
            ],
            compiler_params=pltpu.CompilerParams(collective_id=0, has_side_effects=True),
        )(flux_image, inv_var, pixel_mask, psf_columns, psf_rows, epoch_times, trial_rates))

    in_specs = (
        P("epoch", "row", None),
        P("epoch", "row", None),
        P("epoch", "row", None),
        P("epoch", None),
        P("epoch", None),
        P("epoch"),
        P(),
    )
    out_specs = (P("epoch", "row", None), P("epoch", "row", None))
    return jax.shard_map(
        on_device, mesh=mesh, in_specs=in_specs, out_specs=out_specs, check_vma=False
    )
```

time: 132 us -> 25.2 us (0.19)
  local copies, waits for them, and re-layouts: 52 us -> 3.6 us
  waiting for transfers between devices: 46.3 us -> 0 us
  Pallas kernels: 0 us -> 20.8 us
  between operations: 14.2 us -> 0.65 us
  other arithmetic: 11.6 us -> 0 us
  starting transfers between devices: 6.26 us -> 0 us
    gather x48 -> x0, local copies, waits for them, and re-layouts: 43.5 us -> none
    reduce_scatter x1 -> x0, waiting for transfers between devices: 27.1 us -> none  [on_device(): lax.psum_scatter(shifted_sum(padded, row_starts, column_starts, own_rows)...]
    pallas_call x0 -> x1, Pallas kernels: none -> 20.8 us  [on_device(): pl.pallas_call(functools.partial(kernel, (groups, row_devices)), out_shap...]
    ppermute x2 -> x0, waiting for transfers between devices: 19.2 us -> none  [the longest x1 19.2 us: with_halo(): before = lax.ppermute(last, axis, up)]
    ppermute x2 -> x0, starting transfers between devices: 6.22 us -> none  [the longest x1 4.93 us: with_halo(): before = lax.ppermute(last, axis, up)]
    another operation x8 -> x0, other arithmetic: 4.43 us -> none  [the longest x3 2.68 us: on_device(): jnp.stack([psf_columns, psf_columns * psf_columns], axis=1)]
    add x2 -> x0, other arithmetic: 3.64 us -> none  [the longest x1 3.56 us: conv_columns(): result + kernel[:, :, tap_index][:, :, None, None] * padded[:, :, :, tap_...]
    unnamed x6 -> x5, local copies, waits for them, and re-layouts: 0.02 us -> 3.6 us
  transfers between devices with their start and end apart: 3 -> 0, of which waited for: 2 -> 0; matrix products, arithmetic and copies ran while one was open for 1% -> 0% of each run, Pallas kernels for 0% -> 0%
where the time goes in v1:
time: 25.2 us; the launch traced here: 25 us
  Pallas kernels  20.8 us (83%)
  local copies, waits for them, and re-layouts  3.6 us (14%)
  between operations  0.65 us (3%)
    pallas_call x1, Pallas kernels, on_device(): pl.pallas_call(functools.partial(kernel, (groups, row_devices)), out_shap...  20.8 us
    unnamed x5, local copies, waits for them, and re-layouts  3.6 us

profile of v1, /device:TPU:0, one launch (start us, length us, event | category | flops | bytes accessed | tf_op | source)
XLA Modules:
  0.0 25.0 jit_solution(11827212149041921586)
XLA Ops:
  0.6 1.3 %copy.9.rates = s32[4,2]{1,0:T(4,128)} copy(s32[4,2]{0,1:T(2,128)} %param.13) | data formatting | bytes 64 | tf_op args[6]
  2.0 20.8 %shard_map.86 = (f32[1,32,1024]{2,1,0:T(8,128)}, f32[1,32,1024]{2,1,0:T(8,128)}) custom-call(f32[4,32,1024]{2,1,0:T(8,128)} %flux_hbm.1, f32[4,32,1024]{2,1,0:T(8,128)} %inv_hbm.1, s32[4,32,1024]{2,1,0:T(8,128)} %mask_hbm.1, f32[4,13]{1,0:T(4,128)} %psf_columns.1, f32[4,13]{1,0:T(4,128)} %psf_rows.1, s32[4]{0:T(128)} %times.1, s32[4,2]{1,0:T(4,128)} %copy.9.rates), custom_call_target="tpu_custom_call" | custom-call | tf_op jit(solution)/shard_map/pallas_call | solution.py:301
  22.7 0.0 copy-start
  22.8 1.6 %copy.12 = f32[1,32,1024]{2,1,0:T(8,128)} copy(f32[1,32,1024]{2,1,0:T(8,128)} %get-tuple-element.4) | data formatting | bytes 262144
  24.4 0.0 copy-done
  24.4 0.7 %copy.13 = f32[1,32,1024]{2,1,0:T(8,128)} copy(f32[1,32,1024]{2,1,0:T(8,128)S(1)} %copy-done) | data formatting | bytes 262144
Async XLA Ops:
  22.7 1.6 %copy-start = (f32[1,32,1024]{2,1,0:T(8,128)S(1)}, f32[1,32,1024]{2,1,0:T(8,128)}, u32[]{:S(2)}) copy-start(f32[1,32,1024]{2,1,0:T(8,128)} %get-tuple-element.5) | copy-start | bytes 393220

commit v2 on v1

--- a/solution.py
+++ b/solution.py
@@ -102,12 +102,12 @@
                 padded[e, f, n, :, columns:] = piece
 
     def shift(v, axis, e):
-        return (rates[v, axis] * times[e]) >> (TSPAN.bit_length() - 1)
+        return (rates[axis, v] * times[e]) >> (TSPAN.bit_length() - 1)
 
     def row_matrices(v):
         shape = (OVER + rows + NEAR, depth)
         o, k = iota(shape, 0), iota(shape, 1)
-        far = jnp.where(rates[v, 0] >= 0, -2 * NEAR, rows + NEAR)
+        far = jnp.where(rates[0, v] >= 0, -2 * NEAR, rows + NEAR)
         r = jnp.where(o < NEAR, o - NEAR, rows + o - NEAR)
         r = jnp.where(o >= 2 * NEAR, o - 2 * NEAR + far, r)
         r = jnp.where(o >= OVER, o - OVER, r)
@@ -222,7 +222,7 @@
             before = (d, f)
     finish(*before)
 
-    upward = rates[me, 0] >= 0
+    upward = rates[0, me] >= 0
     for f in range(2):
         total = own_over[0, f]
         for d in range(1, groups):
@@ -300,7 +300,7 @@
         dma = pltpu.SemaphoreType.DMA
         return tuple(pl.pallas_call(
             functools.partial(kernel, (groups, row_devices)),
-            out_shape=[jax.ShapeDtypeStruct((1, rows, columns), F32)] * 2,
+            out_shape=[pltpu.VMEM((1, rows, columns), F32)] * 2,
             in_specs=[hbm] * 3 + [smem] * 4,
             out_specs=[vmem] * 2,
             scratch_shapes=[
@@ -324,7 +324,7 @@
                 dma((2, 2)),
             ],
             compiler_params=pltpu.CompilerParams(collective_id=0, has_side_effects=True),
-        )(flux_image, inv_var, pixel_mask, psf_columns, psf_rows, epoch_times, trial_rates))
+        )(flux_image, inv_var, pixel_mask, psf_columns, psf_rows, epoch_times, trial_rates.T))
 
     in_specs = (
         P("epoch", "row", None),

time: 25.2 us -> 22.2 us (0.88)
  local copies, waits for them, and re-layouts: 3.6 us -> 1.31 us
  Pallas kernels: 20.8 us -> 20.1 us
    unnamed x5 -> x2, local copies, waits for them, and re-layouts: 3.6 us -> 1.31 us
    pallas_call x1, Pallas kernels: 20.8 us -> 20.1 us  [on_device(): pl.pallas_call(functools.partial(kernel, (groups, row_devices)), out_shap...]
where the time goes in v2:
time: 22.2 us; the launch traced here: 22 us
  Pallas kernels  20.1 us (91%)
  local copies, waits for them, and re-layouts  1.31 us (6%)
  between operations  0.64 us (3%)
    pallas_call x1, Pallas kernels, on_device(): pl.pallas_call(functools.partial(kernel, (groups, row_devices)), out_shap...  20.1 us
    unnamed x2, local copies, waits for them, and re-layouts  1.31 us

profile of v2, /device:TPU:0, one launch (start us, length us, event | category | flops | bytes accessed | tf_op | source)
XLA Modules:
  0.0 22.0 jit_solution(5158738052769434021)
XLA Ops:
  0.6 20.1 %shard_map.86 = (f32[1,32,1024]{2,1,0:T(8,128)S(1)}, f32[1,32,1024]{2,1,0:T(8,128)S(1)}) custom-call(f32[4,32,1024]{2,1,0:T(8,128)} %flux_hbm.1, f32[4,32,1024]{2,1,0:T(8,128)} %inv_hbm.1, s32[4,32,1024]{2,1,0:T(8,128)} %mask_hbm.1, f32[4,13]{1,0:T(4,128)} %psf_columns.1, f32[4,13]{1,0:T(4,128)} %psf_rows.1, s32[4]{0:T(128)} %times.1, s32[2,4]{1,0:T(2,128)} %bitcast.1), custom_call_target="tpu_custom_call" | custom-call | tf_op jit(solution)/shard_map/pallas_call | solution.py:301
  20.7 0.7 %copy.11 = f32[1,32,1024]{2,1,0:T(8,128)} copy(f32[1,32,1024]{2,1,0:T(8,128)S(1)} %get-tuple-element.2) | data formatting | bytes 262144
  21.4 0.7 %copy.12 = f32[1,32,1024]{2,1,0:T(8,128)} copy(f32[1,32,1024]{2,1,0:T(8,128)S(1)} %get-tuple-element.3) | data formatting | bytes 262144

commit v3 on v2

--- a/solution.py
+++ b/solution.py
@@ -190,37 +190,40 @@
             device_id={"row": other}, device_id_type=MESH,
         )
 
-    def finish(d, f):
-        for part, (own, arrived) in enumerate(((own_over, pair_in_over), (own_mid, pair_in_mid))):
-            pair_copy(d, f, part).wait_recv()
-            own[d, f] = own[d, f] + arrived[d, f]
-            if d:
-                far_copy(d, f, part).start()
+    def finish(d, f, part):
+        own, arrived = ((own_over, pair_in_over), (own_mid, pair_in_mid))[part]
+        pair_copy(d, f, part).wait_recv()
+        own[d, f] = own[d, f] + arrived[d, f]
+        if d:
+            far_copy(d, f, part).start()
 
     order = list(range(1, groups)) + [0]
-    before = None
+    waiting = []
+    entered = False
     for d in order:
         goal = 2 * lax.rem(group + d, groups)
         pair = (goal + 1 - core, goal + core)
         matrices = [row_matrices(v) for v in pair]
         for f in range(2):
             columns_stage(pair, f)
-            if before is None:
+            if not entered:
                 above = lax.div(row + row_devices - 1, row_devices)
                 below = lax.div(2 * row_devices - 2 - row, row_devices)
                 pl.semaphore_wait(barrier, groups + above + below)
-            else:
-                finish(*before)
+                entered = True
+            for n in waiting:
+                finish(*n)
             part = rows_stage(0, matrices[0][f])
             pair_out_over[d, f] = part[:OVER]
+            pair_copy(d, f, 0).start()
             pair_out_mid[d, f] = part[OVER : OVER + rows]
-            pair_copy(d, f, 0).start()
             pair_copy(d, f, 1).start()
             part = rows_stage(1, matrices[1][f])
             own_over[d, f] = part[:OVER]
             own_mid[d, f] = part[OVER : OVER + rows]
-            before = (d, f)
-    finish(*before)
+            waiting = [(d, f, 0)] if f == 0 else [(d, 1, 0), (d, 0, 1), (d, 1, 1)]
+    for n in waiting[:1]:
+        finish(*n)
 
     upward = rates[0, me] >= 0
     for f in range(2):
@@ -242,6 +245,8 @@
         def _():
             row_copy(f, 1, row + 1).start()
 
+    for f in range(2):
+        finish(0, f, 1)
         total = own_mid[0, f]
         for d in range(1, groups):
             far_copy(d, f, 1).wait_recv()

time: 22.2 us -> 21 us (0.946)
  Pallas kernels: 20.1 us -> 18.8 us
    pallas_call x1, Pallas kernels: 20.1 us -> 18.8 us  [on_device(): pl.pallas_call(functools.partial(kernel, (groups, row_devices)), out_shap...]
where the time goes in v3:
time: 21 us; the launch traced here: 20.8 us
  Pallas kernels  18.8 us (90%)
  local copies, waits for them, and re-layouts  1.31 us (6%)
  between operations  0.64 us (3%)
    pallas_call x1, Pallas kernels, on_device(): pl.pallas_call(functools.partial(kernel, (groups, row_devices)), out_shap...  18.8 us
    unnamed x2, local copies, waits for them, and re-layouts  1.31 us

profile of v3, /device:TPU:0, one launch (start us, length us, event | category | flops | bytes accessed | tf_op | source)
XLA Modules:
  0.0 20.8 jit_solution(6359978037066882043)
XLA Ops:
  0.6 18.8 %shard_map.86 = (f32[1,32,1024]{2,1,0:T(8,128)S(1)}, f32[1,32,1024]{2,1,0:T(8,128)S(1)}) custom-call(f32[4,32,1024]{2,1,0:T(8,128)} %flux_hbm.1, f32[4,32,1024]{2,1,0:T(8,128)} %inv_hbm.1, s32[4,32,1024]{2,1,0:T(8,128)} %mask_hbm.1, f32[4,13]{1,0:T(4,128)} %psf_columns.1, f32[4,13]{1,0:T(4,128)} %psf_rows.1, s32[4]{0:T(128)} %times.1, s32[2,4]{1,0:T(2,128)} %bitcast.1), custom_call_target="tpu_custom_call" | custom-call | tf_op jit(solution)/shard_map/pallas_call | solution.py:306
  19.5 0.7 %copy.11 = f32[1,32,1024]{2,1,0:T(8,128)} copy(f32[1,32,1024]{2,1,0:T(8,128)S(1)} %get-tuple-element.2) | data formatting | bytes 262144
  20.1 0.7 %copy.12 = f32[1,32,1024]{2,1,0:T(8,128)} copy(f32[1,32,1024]{2,1,0:T(8,128)S(1)} %get-tuple-element.3) | data formatting | bytes 262144
